TPU v7x, 512 devices: a whole 4x4x16 slice. The times are simulated.
512 devices in a mesh: pages: 128 (over x, z, core), mp: 4 (over y).
Axes of the slice: x: 4, y: 4, z: 16, core: 2. Of those that a mesh axis runs over, the one named last changes fastest.
Arguments:
- queries: bfloat16 [256, 8192], P('pages', 'mp'), may hold values from -9 to 9
- cached_keys: bfloat16 [2048, 128, 8, 128], P('pages', None, 'mp'), may hold values from -8 to 8
- cached_values: bfloat16 [2048, 128, 8, 128], P('pages', None, 'mp'), may hold values from -4 to 4
- out_weight: bfloat16 [8192, 8192], P('mp', 'pages'), may hold values from -0.0625 to 0.0625
- select: int32 [2, 24], replicated, may hold values from 0 to 2047, as said below
- page_table: int32 [2048], replicated, may hold values from 0 to 2047, as said below
- block_page: int32 [2], replicated, may hold values from 0 to 2047, as said below
Outputs:
- mixed: bfloat16 [256, 8192], P('mp', 'pages')
Inputs may be any that keep to these rules, and one draw needn't show every extreme that they name: A permutation: each logical page has its own cache row, held by index page_table[p] // 16 of pages. `select`: each row holds 24 distinct pages: the block's own page block_page[b] and pages lying wholly before the block. They lie on exactly 4 owners, 6 on each. No owner holds selected pages of more than min(2, 4) blocks, and some owner holds that many. `block_page`: Distinct.
All inputs are finite; a program needn't handle non-finite values.
Results may differ from a plain program's by a relative error of at most 0.0063.
Values may be sent and summed in bfloat16 or wider, within the bound.
A program may use at most 64 MiB of HBM per device.

v0:
```python
import jax
import jax.numpy as jnp
from jax import lax
from jax.experimental import pallas as pl
from jax.experimental.pallas import tpu as pltpu
from jax.sharding import Mesh
from jax.sharding import PartitionSpec as P

PAGES = ("x", "z", "c")
MESH = pl.DeviceIdType.MESH
NX, NZ, NY = 4, 16, 4
PAGE = 128
PAGES_DEV = 16
PICKED = 6
BLOCKS = 2
HEADS = 8
HEAD = 128
KEYS = PICKED * PAGE
SCALE = HEAD ** -0.5
FLOOR = -1e30
VMEM = pltpu.MemorySpace.VMEM
DMA = pltpu.SemaphoreType.DMA
TERM = jnp.bfloat16


def around(value, size):
    return lax.rem(value + size, size)


def place():
    return tuple(lax.axis_index(axis) for axis in ("x", "z", "c", "y"))


def greet(peers):
    barrier = pltpu.get_barrier_semaphore()
    for peer in peers:
        pl.semaphore_signal(barrier, inc=1, device_id=peer, device_id_type=MESH)
    pl.semaphore_wait(barrier, len(peers))


def sent(source, target, send_sem, recv_sem, peer):
    return pltpu.make_async_remote_copy(
        src_ref=source,
        dst_ref=target,
        send_sem=send_sem,
        recv_sem=recv_sem,
        device_id=peer,
        device_id_type=MESH,
    )


def arrived(target, sem):
    pltpu.make_async_copy(target, target, sem).wait()


def nearest(reverse=False):
    found = [hop for step in range(1, NZ // 2) for hop in (step, NZ - step)] + [NZ // 2]
    return found[::-1] if reverse else found


def blended(items):
    top = items[0][1]
    for _, level in items[1:]:
        top = jnp.maximum(top, level)
    shares = [jnp.exp(level - top) for _, level in items]
    total = shares[0]
    for share in shares[1:]:
        total = total + share
    scale = 1.0 / total
    lines = [[None, None], [None, None]]
    for (value, _), share in zip(items, shares):
        share = share * scale
        for band in range(2):
            for half in range(2):
                lane = band * 64 + half * 32
                term = value[band * 8:(band + 1) * 8, half * HEAD:(half + 1) * HEAD] * share[:, lane:lane + 1]
                before = lines[band][half]
                lines[band][half] = term if before is None else before + term
    value = jnp.concatenate([jnp.concatenate(line, axis=1) for line in lines], axis=0)
    return value, top + jnp.log(total)


def listed(select, table, block_page, lists, chip, c):
    for block in range(BLOCKS):
        own_page = block_page[block]
        own_row = table[own_page]
        for side in range(2):
            owner = chip * 2 + (c if side == 0 else 1 - c)
            has_own = (lax.shift_right_logical(own_row, 4) == owner).astype(jnp.int32)
            spots = [jnp.where(has_own == 1, own_row & (PAGES_DEV - 1), 0)] + [jnp.int32(0)] * (PICKED - 1)

            def scan(i, carry, block=block, owner=owner, own_page=own_page):
                count, *spots = carry
                page = select[block, i]
                row = table[page]
                hit = jnp.logical_and(lax.shift_right_logical(row, 4) == owner, page != own_page)
                spots = [
                    jnp.where(jnp.logical_and(hit, count == n), row & (PAGES_DEV - 1), spot)
                    for n, spot in enumerate(spots)
                ]
                return (count + hit.astype(jnp.int32), *spots)

            count, *spots = lax.fori_loop(0, 4 * PICKED, scan, (has_own, *spots))
            base = (block * 2 + side) * 8
            for n, spot in enumerate(spots):
                lists[base + n] = spot
            lists[base + PICKED] = count
            lists[base + PICKED + 1] = has_own


def step_kernel(
    select, table, block_page, q, k, v, w, result,
    lists, qall, knear, vnear, kfar, vfar, flat, keys, values, acc, tops, part, stat, got, got_stat,
    send, send_stat, land, land_stat, merged, wz, terms, terms_in, lines,
    ls, ps, pr, zs, zr, xs, xr, ws, wr, gs, gr, hs, hr, rs, rr, ts, tr, ms, mr, fs, fr,
):
    x, z, c, y = place()
    here = x * 2 + c
    other = {"c": 1 - c}
    xpeers = [{"x": around(x + j, NX)} for j in range(1, NX)]
    near = [{"x": around(x + j, NX), "c": lax.rem(c + d, 2)} for j in range(NX) for d in range(2)][1:]
    zero = jnp.zeros((2 * NX, 64, 256), jnp.bfloat16)
    wz[:, :64, 256:] = zero
    wz[:, 64:, :256] = zero
    peers = [{"z": around(z + hop, NZ), "c": core} for hop in nearest(True) for core in range(2)] + near
    for j in range(1, NY):
        for peer in [{"x": x, "c": c}] + near:
            peers.append({"y": around(y + j, NY), **peer})
    own = [
        pltpu.make_async_copy(k, knear, ls.at[0]),
        pltpu.make_async_copy(v, vnear, ls.at[1]),
        pltpu.make_async_copy(q.at[c], qall.at[x, z, c], ls.at[2]),
    ]
    mine = pl.multiple_of((c * NX + x) * 256, 256)
    for n in range(2):
        own.append(pltpu.make_async_copy(
            w.at[:, pl.ds(mine, 256)], wz.at[here, pl.ds(64 * n, 64), pl.ds(256 * n, 256)], ls.at[3 + n]
        ))
    for copy in own:
        copy.start()
    greet(peers)
    started = []

    def go(copy):
        copy.start()
        started.append(copy)

    for hop in nearest(True):
        for core in range(2):
            peer = {"z": around(z + hop, NZ), "c": core}
            go(sent(q.at[core], qall.at[x, z, c], zs.at[hop, core], zr.at[hop, c], peer))
    go(sent(q.at[1 - c], qall.at[x, z, c], zs.at[0, 0], zr.at[0, c], other))
    go(sent(k, kfar, ps.at[0], pr.at[0], other))
    go(sent(v, vfar, ps.at[1], pr.at[1], other))

    def across(slot, number):
        for j in range(1, NX):
            go(sent(qall.at[x, slot], qall.at[x, slot], xs.at[j - 1, number], xr.at[j - 1, slot], xpeers[j - 1]))

    listed(select, table, block_page, lists, x * NZ + z, c)
    for copy in own:
        copy.wait()
    arrived(qall.at[x, z, 1 - c], zr.at[0, 1 - c])
    across(z, 0)

    def untangle(side, raws):
        def one(i, _, side=side):
            for block in range(BLOCKS):
                row = lists[(block * 2 + side) * 8 + i]
                at = pl.ds(pl.multiple_of(i * PAGE, PAGE), PAGE)
                for n, (raw, kept) in enumerate(zip(raws, (keys, values))):
                    spot = block * 2 + n
                    flat[spot] = raw[row].astype(jnp.float32)
                    kept[block * 2 + side, at, :] = flat[spot, pl.ds(c, PAGE, stride=2), :].astype(jnp.bfloat16)
            return 0

        lax.fori_loop(0, PICKED, one, 0)

    untangle(0, (knear, vnear))
    for number, hop in enumerate(nearest()):
        slot = around(z - hop, NZ)
        arrived(qall.at[x, slot, 0], zr.at[hop, 0])
        arrived(qall.at[x, slot, 1], zr.at[hop, 1])
        across(slot, 1 + number)
    for number, peer in enumerate(near):
        xd, cd = peer["x"], peer["c"]
        theirs = pl.multiple_of((cd * NX + xd) * 256, 256)
        for n in range(2):
            go(sent(
                w.at[:, pl.ds(theirs, 256)],
                wz.at[here, pl.ds(64 * n, 64), pl.ds(256 * n, 256)],
                ws.at[number, n], wr.at[here, n], peer,
            ))
    arrived(kfar, pr.at[0])
    arrived(vfar, pr.at[1])
    untangle(1, (kfar, vfar))
    lane = lax.broadcasted_iota(jnp.int32, (2, 8, HEAD), 2)
    size = 256

    def group(xg):
        block = xg // 2
        away = around(x - xg, NX)

        @pl.when(away != 0)
        def _():
            for slot in range(NZ):
                arrived(qall.at[xg, slot], xr.at[away - 1, slot])

        for tile in range(2):
            rows = pl.ds(tile * size, size)
            queries = qall[xg, tile * 8:tile * 8 + 8].reshape(size, HEAD)
            sides = []
            for side in range(2):
                combo = block * 2 + side
                scores = lax.dot_general(
                    queries, keys[combo], (((1,), (1,)), ((), ())), preferred_element_type=jnp.float32
                )
                slack = jnp.where(lists[combo * 8 + PICKED + 1] == 1, 0, PAGE)
                line = lax.broadcasted_iota(jnp.int32, (size, PAGE), 0) + tile * size
                row = lax.shift_left(lax.shift_right_logical(line, 4), 1) + (line & 1) + xg % 2 * 64
                key = lax.broadcasted_iota(jnp.int32, (size, PAGE), 1)
                first = jnp.where(key <= row + slack, scores[:, :PAGE], FLOOR)
                scores = jnp.concatenate([first, scores[:, PAGE:]], axis=1)
                peak = jnp.max(scores, axis=1, keepdims=True)
                weights = jnp.exp((scores - peak) * SCALE)
                total = jnp.sum(weights, axis=1, keepdims=True)
                out = jnp.dot(weights.astype(jnp.bfloat16), values[combo], preferred_element_type=jnp.float32)
                level = peak * SCALE + jnp.log(total)
                level = jnp.where(lists[combo * 8 + PICKED] == PICKED, level, FLOOR)
                sides.append((out, total, level))
            top = jnp.maximum(sides[0][2], sides[1][2])
            shares = [jnp.exp(level - top) for _, _, level in sides]
            whole = shares[0] + shares[1]
            acc[rows, :] = sum(
                out * (share / (whole * total)) for (out, total, _), share in zip(sides, shares)
            )
            tops[rows, :] = jnp.broadcast_to(top + jnp.log(whole), (size, HEAD))
        for xd in range(NX):
            for r in range(2):
                at = slice(4 * xg + 2 * r, 4 * xg + 2 * r + 2)
                pieces = []
                for half in range(2):
                    start = (2 * xd + half) * 2 + r
                    piece = acc[pl.ds(start, 32, stride=16), :].astype(jnp.bfloat16)
                    part[xd, at, :, half * HEAD:(half + 1) * HEAD] = piece.reshape(2, 16, HEAD)
                    pieces.append(tops[pl.ds(start, 32, stride=16), :].reshape(2, 16, HEAD))
                low = jnp.where(lane < 32, pieces[0][:, :8], pieces[1][:, :8])
                high = jnp.where(lane < 96, pieces[0][:, 8:], pieces[1][:, 8:])
                stat[xd, at] = jnp.where(lane < 64, low, high)
        at = pl.ds(4 * xg, 4)
        for j in range(1, NX):
            xd = around(x + j, NX)
            go(sent(stat.at[xd, at], got_stat.at[j - 1, at], hs.at[j - 1, xg], hr.at[j - 1, xg], xpeers[j - 1]))
            go(sent(part.at[xd, at], got.at[j - 1, at], gs.at[j - 1, xg], gr.at[j - 1, xg], xpeers[j - 1]))

    def along(slot, value, level):
        peer = {"z": jnp.int32(slot)}
        return [
            sent(send_stat.at[slot], land_stat.at[z], ts.at[slot], tr.at[z], peer),
            sent(send.at[slot], land.at[z], rs.at[slot], rr.at[z], peer),
        ]

    def combine(xg):
        at = pl.ds(4 * xg, 4)
        for j in range(NX - 1):
            arrived(got_stat.at[j, at], hr.at[j, xg])
            arrived(got.at[j, at], gr.at[j, xg])
        for slot in range(4 * xg, 4 * xg + 4):
            items = [(part[x, slot].astype(jnp.float32), stat[x, slot])]
            for j in range(NX - 1):
                items.append((got[j, slot].astype(jnp.float32), got_stat[j, slot]))
            value, level = blended(items)

            @pl.when(z == slot)
            def _(value=value, level=level):
                land[z] = value.astype(jnp.bfloat16)
                land_stat[z] = level

            @pl.when(z != slot)
            def _(value=value, level=level, slot=slot):
                send[slot] = value.astype(jnp.bfloat16)
                send_stat[slot] = level
                for copy in along(slot, value, level):
                    copy.start()

    group(0)
    group(1)
    combine(0)
    group(2)
    combine(1)
    group(3)
    combine(2)
    combine(3)
    for hop in nearest():
        slot = around(z - hop, NZ)
        arrived(land_stat.at[slot], tr.at[slot])
        arrived(land.at[slot], rr.at[slot])
    items = [(land[slot].astype(jnp.float32), land_stat[slot]) for slot in range(NZ)]
    merged[z] = blended(items)[0].astype(jnp.bfloat16)
    for hop in nearest(True):
        go(sent(merged.at[z], merged.at[z], ms.at[hop], mr.at[hop], {"z": around(z + hop, NZ)}))
    for number, peer in enumerate(near):
        there = peer["x"] * 2 + peer["c"]
        for n in range(2):
            arrived(wz.at[there, pl.ds(64 * n, 64), pl.ds(256 * n, 256)], wr.at[there, n])
    for hop in nearest():
        arrived(merged.at[around(z - hop, NZ)], mr.at[hop])
    rows = merged[...].reshape(NY, 2, 32, 256)
    rows = jnp.concatenate([rows[:, 0].reshape(128, 256), rows[:, 1].reshape(128, 256)], axis=1)
    for spot in range(2 * NX):
        term = lax.dot_general(rows, wz[spot], (((1,), (1,)), ((), ())), preferred_element_type=jnp.float32)
        terms[spot] = term.reshape(NY, 32, 128).astype(TERM)
    number = 0
    for j in range(NY)[::-1]:
        for peer in ([] if j == 0 else [{"x": x, "c": c}]) + near:
            yd = around(y + j, NY)
            spot = peer["x"] * 2 + peer["c"]
            mark = y * 8 + here
            go(sent(terms.at[spot, yd], terms_in.at[mark], fs.at[number], fr.at[mark], {"y": yd, **peer}))
            number += 1
    total = terms[here, y].astype(jnp.float32)
    for j in range(NY):
        for peer in ([] if j == 0 else [{"x": x, "c": c}]) + near:
            mark = around(y + j, NY) * 8 + peer["x"] * 2 + peer["c"]
            arrived(terms_in.at[mark], fr.at[mark])
            total = total + terms_in[mark].astype(jnp.float32)
    lines[pl.ds(0, 32, stride=2), :] = total
    lines[pl.ds(1, 32, stride=2), :] = jnp.concatenate([total[:, 64:], total[:, :64]], axis=1)
    result[...] = lines[:, :64].astype(jnp.bfloat16)
    for copy in started:
        copy.wait_send()
    for slot in range(NZ):

        @pl.when(z != slot)
        def _(slot=slot):
            for copy in along(slot, None, None):
                copy.wait_send()


def step(select, table, block_page, q, k, v, w):
    anywhere = pl.BlockSpec(memory_space=pl.ANY)
    inside = pl.BlockSpec(memory_space=VMEM)
    scalars = pl.BlockSpec(memory_space=pltpu.MemorySpace.SMEM)
    half = lambda *shape: pltpu.VMEM(shape, jnp.bfloat16)
    full = lambda *shape: pltpu.VMEM(shape, jnp.float32)
    pages = (PAGES_DEV, 2 * PAGE, HEAD)
    return pl.pallas_call(
        step_kernel,
        out_shape=jax.ShapeDtypeStruct((64, 64), jnp.bfloat16),
        in_specs=[scalars] * 3 + [inside] + [anywhere] * 3,
        out_specs=inside,
        scratch_shapes=[
            pltpu.SMEM((BLOCKS * 2 * 8,), jnp.int32),
            half(NX, NZ, 2, 16, HEAD),
            half(*pages), half(*pages), half(*pages), half(*pages),
            full(4, 2 * PAGE, HEAD),
            half(4, KEYS, HEAD), half(4, KEYS, HEAD),
            full(512, HEAD), full(512, HEAD),
            half(NX, NZ, 16, 256), full(NX, NZ, 8, HEAD),
            half(NX - 1, NZ, 16, 256), full(NX - 1, NZ, 8, HEAD),
            half(NZ, 16, 256), full(NZ, 8, HEAD),
            half(NZ, 16, 256), full(NZ, 8, HEAD),
            half(NZ, 16, 256),
            half(2 * NX, 128, 512),
            pltpu.VMEM((2 * NX, NY, 32, 128), TERM),
            pltpu.VMEM((8 * NY, 32, 128), TERM),
            full(64, 128),
            DMA((5,)), DMA((2,)), DMA((2,)),
            DMA((NZ, 2)), DMA((NZ, 2)), DMA((NX - 1, NZ)), DMA((NX - 1, NZ)),
            DMA((7, 2)), DMA((8, 2)),
            DMA((NX - 1, NX)), DMA((NX - 1, NX)), DMA((NX - 1, NX)), DMA((NX - 1, NX)),
            DMA((NZ,)), DMA((NZ,)), DMA((NZ,)), DMA((NZ,)),
            DMA((NZ,)), DMA((NZ,)),
            DMA((31,)), DMA((32,)),
        ],
        compiler_params=pltpu.CompilerParams(collective_id=0, has_side_effects=True),
        name="step",
    )(select, table, block_page, q, k, v, w)


def per_device(queries, cached_keys, cached_values, out_weight, select, page_table, block_page):
    q = queries.reshape(2, 2 * HEADS, HEAD).transpose(1, 0, 2).reshape(2, 16, HEAD)
    k = cached_keys.reshape(PAGES_DEV, 2 * PAGE, HEAD)
    v = cached_values.reshape(PAGES_DEV, 2 * PAGE, HEAD)
    return step(select, page_table, block_page, q, k, v, out_weight.T)


def solution(mesh):
    torus = Mesh(mesh.devices.reshape(NX, NZ, 2, NY), ("x", "z", "c", "y"))
    return jax.shard_map(
        per_device,
        mesh=torus,
        in_specs=(
            P(PAGES, "y"),
            P(PAGES, None, "y", None),
            P(PAGES, None, "y", None),
            P("y", PAGES),
            P(),
            P(),
            P(),
        ),
        out_specs=P("y", PAGES),
        check_vma=False,
    )
```

profile of v0, /device:TPU:1, one launch (start us, length us, event | category | flops | bytes accessed | tf_op | source)
XLA Modules:
  0.0 83.5 jit_solution(9477388642196932011)
XLA Ops:
  0.0 82.2 %step.1 = bf16[64,64]{1,0:T(8,128)(2,1)} custom-call(s32[2,24]{1,0:T(2,128)} %select.1, s32[2048]{0:T(1024)} %table.1, s32[2]{0:T(128)} %block_page.1, bf16[2,16,128]{2,1,0:T(8,128)(2,1)} %bitcast.11, bf16[16,256,128]{2,1,0:T(8,128)(2,1)} %bitcast.8, bf16[16,256,128]{2,1,0:T(8,128)(2,1)} %bitcast.9, bf16[64,2048]{1,0:T(8,128)(2,1)} %bitcast.10), custom_call_target="tpu_custom_call" | custom-call | tf_op jit(solution)/shard_map/step/pallas_call | solution.py:347
  82.2 1.3 %copy.10 = bf16[64,64]{1,0:T(8,128)(2,1)} copy(bf16[64,64]{1,0:T(8,128)(2,1)} %step.1) | data formatting | bytes 16384
where the time goes:
time: 83.7 us; the launch traced here: 83.5 us
  Pallas kernels  82.2 us (98%)
  local copies, waits for them, and re-layouts  1.32 us (2%)
    pallas_call x1, Pallas kernels, step(): pl.pallas_call(step_kernel, out_shape=jax.ShapeDtypeStruct((64, 64), jnp....  82.2 us

commit v1 on v0

--- a/solution.py
+++ b/solution.py
@@ -35,7 +35,7 @@
     barrier = pltpu.get_barrier_semaphore()
     for peer in peers:
         pl.semaphore_signal(barrier, inc=1, device_id=peer, device_id_type=MESH)
-    pl.semaphore_wait(barrier, len(peers))
+    return lambda: pl.semaphore_wait(barrier, len(peers))
 
 
 def sent(source, target, send_sem, recv_sem, peer):
@@ -58,26 +58,31 @@
     return found[::-1] if reverse else found
 
 
-def blended(items):
-    top = items[0][1]
-    for _, level in items[1:]:
+def weighed(levels):
+    top = levels[0]
+    for level in levels[1:]:
         top = jnp.maximum(top, level)
-    shares = [jnp.exp(level - top) for _, level in items]
+    shares = [jnp.exp(level - top) for level in levels]
     total = shares[0]
     for share in shares[1:]:
         total = total + share
     scale = 1.0 / total
-    lines = [[None, None], [None, None]]
-    for (value, _), share in zip(items, shares):
-        share = share * scale
-        for band in range(2):
-            for half in range(2):
-                lane = band * 64 + half * 32
+    return [share * scale for share in shares], top + jnp.log(total)
+
+
+def mixed_by(values, shares, base):
+    lines = []
+    for band in range(2):
+        line = []
+        for half in range(2):
+            lane = base + 8 * (band * 2 + half)
+            total = None
+            for value, share in zip(values, shares):
                 term = value[band * 8:(band + 1) * 8, half * HEAD:(half + 1) * HEAD] * share[:, lane:lane + 1]
-                before = lines[band][half]
-                lines[band][half] = term if before is None else before + term
-    value = jnp.concatenate([jnp.concatenate(line, axis=1) for line in lines], axis=0)
-    return value, top + jnp.log(total)
+                total = term if total is None else total + term
+            line.append(total)
+        lines.append(jnp.concatenate(line, axis=1))
+    return jnp.concatenate(lines, axis=0)
 
 
 def listed(select, table, block_page, lists, chip, c):
@@ -109,59 +114,53 @@
 
 
 def step_kernel(
-    select, table, block_page, q, k, v, w, result,
-    lists, qall, knear, vnear, kfar, vfar, flat, keys, values, acc, tops, part, stat, got, got_stat,
-    send, send_stat, land, land_stat, merged, wz, terms, terms_in, lines,
+    select_in, table_in, block_page_in, q_in, k, v, w, result,
+    select, table, block_page, lists, q, qall, knear, vnear, kfar, vfar, flat, keys, values, acc, tops,
+    part, stat, got, got_stat, send, send_stat, land, land_stat, merged, wz, terms, terms_in, lines,
     ls, ps, pr, zs, zr, xs, xr, ws, wr, gs, gr, hs, hr, rs, rr, ts, tr, ms, mr, fs, fr,
 ):
     x, z, c, y = place()
     here = x * 2 + c
     other = {"c": 1 - c}
     xpeers = [{"x": around(x + j, NX)} for j in range(1, NX)]
-    near = [{"x": around(x + j, NX), "c": lax.rem(c + d, 2)} for j in range(NX) for d in range(2)][1:]
+    around_me = [{"x": around(x + j, NX), "c": lax.rem(c + d, 2)} for j in range(NX) for d in range(2)]
+    near = around_me[1:]
+    peers = [{"z": around(z + hop, NZ), "c": core} for hop in nearest(True) for core in range(2)] + near
+    for j in range(1, NY):
+        for peer in around_me:
+            peers.append({"y": around(y + j, NY), **peer})
+    wait_for_all = greet(peers)
+    mine = pl.multiple_of((c * NX + x) * 256, 256)
+    own = [
+        pltpu.make_async_copy(select_in, select, ls.at[0]),
+        pltpu.make_async_copy(table_in, table, ls.at[1]),
+        pltpu.make_async_copy(block_page_in, block_page, ls.at[2]),
+        pltpu.make_async_copy(q_in, q, ls.at[3]),
+        pltpu.make_async_copy(k, knear, ls.at[4]),
+        pltpu.make_async_copy(v, vnear, ls.at[5]),
+        pltpu.make_async_copy(w.at[:, pl.ds(mine, 256)], wz.at[here, pl.ds(0, 64), pl.ds(0, 256)], ls.at[6]),
+    ]
+    for copy in own:
+        copy.start()
+    for copy in own[:4]:
+        copy.wait()
+    copy = pltpu.make_async_copy(q.at[c], qall.at[x, z, c], ls.at[7])
+    copy.start()
     zero = jnp.zeros((2 * NX, 64, 256), jnp.bfloat16)
     wz[:, :64, 256:] = zero
     wz[:, 64:, :256] = zero
-    peers = [{"z": around(z + hop, NZ), "c": core} for hop in nearest(True) for core in range(2)] + near
-    for j in range(1, NY):
-        for peer in [{"x": x, "c": c}] + near:
-            peers.append({"y": around(y + j, NY), **peer})
-    own = [
-        pltpu.make_async_copy(k, knear, ls.at[0]),
-        pltpu.make_async_copy(v, vnear, ls.at[1]),
-        pltpu.make_async_copy(q.at[c], qall.at[x, z, c], ls.at[2]),
-    ]
-    mine = pl.multiple_of((c * NX + x) * 256, 256)
-    for n in range(2):
-        own.append(pltpu.make_async_copy(
-            w.at[:, pl.ds(mine, 256)], wz.at[here, pl.ds(64 * n, 64), pl.ds(256 * n, 256)], ls.at[3 + n]
-        ))
-    for copy in own:
-        copy.start()
-    greet(peers)
+    listed(select, table, block_page, lists, x * NZ + z, c)
+    for copy in own[4:] + [copy]:
+        copy.wait()
     started = []
 
     def go(copy):
         copy.start()
         started.append(copy)
 
-    for hop in nearest(True):
-        for core in range(2):
-            peer = {"z": around(z + hop, NZ), "c": core}
-            go(sent(q.at[core], qall.at[x, z, c], zs.at[hop, core], zr.at[hop, c], peer))
-    go(sent(q.at[1 - c], qall.at[x, z, c], zs.at[0, 0], zr.at[0, c], other))
-    go(sent(k, kfar, ps.at[0], pr.at[0], other))
-    go(sent(v, vfar, ps.at[1], pr.at[1], other))
-
     def across(slot, number):
         for j in range(1, NX):
             go(sent(qall.at[x, slot], qall.at[x, slot], xs.at[j - 1, number], xr.at[j - 1, slot], xpeers[j - 1]))
-
-    listed(select, table, block_page, lists, x * NZ + z, c)
-    for copy in own:
-        copy.wait()
-    arrived(qall.at[x, z, 1 - c], zr.at[0, 1 - c])
-    across(z, 0)
 
     def untangle(side, raws):
         def one(i, _, side=side):
@@ -177,24 +176,29 @@
         lax.fori_loop(0, PICKED, one, 0)
 
     untangle(0, (knear, vnear))
+    wait_for_all()
+    for hop in nearest(True):
+        for core in range(2):
+            peer = {"z": around(z + hop, NZ), "c": core}
+            go(sent(q.at[core], qall.at[x, z, c], zs.at[hop, core], zr.at[hop, c], peer))
+    go(sent(q.at[1 - c], qall.at[x, z, c], zs.at[0, 0], zr.at[0, c], other))
+    go(sent(knear, kfar, ps.at[0], pr.at[0], other))
+    go(sent(vnear, vfar, ps.at[1], pr.at[1], other))
+    for number, peer in enumerate(near):
+        theirs = pl.multiple_of((peer["c"] * NX + peer["x"]) * 256, 256)
+        target = wz.at[here, pl.ds(0, 64), pl.ds(0, 256)]
+        go(sent(w.at[:, pl.ds(theirs, 256)], target, ws.at[number], wr.at[here], peer))
+    arrived(qall.at[x, z, 1 - c], zr.at[0, 1 - c])
+    across(z, 0)
     for number, hop in enumerate(nearest()):
         slot = around(z - hop, NZ)
         arrived(qall.at[x, slot, 0], zr.at[hop, 0])
         arrived(qall.at[x, slot, 1], zr.at[hop, 1])
         across(slot, 1 + number)
-    for number, peer in enumerate(near):
-        xd, cd = peer["x"], peer["c"]
-        theirs = pl.multiple_of((cd * NX + xd) * 256, 256)
-        for n in range(2):
-            go(sent(
-                w.at[:, pl.ds(theirs, 256)],
-                wz.at[here, pl.ds(64 * n, 64), pl.ds(256 * n, 256)],
-                ws.at[number, n], wr.at[here, n], peer,
-            ))
     arrived(kfar, pr.at[0])
     arrived(vfar, pr.at[1])
     untangle(1, (kfar, vfar))
-    lane = lax.broadcasted_iota(jnp.int32, (2, 8, HEAD), 2)
+    lane = lax.broadcasted_iota(jnp.int32, (8, HEAD), 1)
     size = 256
 
     def group(xg):
@@ -236,6 +240,7 @@
             )
             tops[rows, :] = jnp.broadcast_to(top + jnp.log(whole), (size, HEAD))
         for xd in range(NX):
+            tile = None
             for r in range(2):
                 at = slice(4 * xg + 2 * r, 4 * xg + 2 * r + 2)
                 pieces = []
@@ -243,17 +248,18 @@
                     start = (2 * xd + half) * 2 + r
                     piece = acc[pl.ds(start, 32, stride=16), :].astype(jnp.bfloat16)
                     part[xd, at, :, half * HEAD:(half + 1) * HEAD] = piece.reshape(2, 16, HEAD)
-                    pieces.append(tops[pl.ds(start, 32, stride=16), :].reshape(2, 16, HEAD))
-                low = jnp.where(lane < 32, pieces[0][:, :8], pieces[1][:, :8])
-                high = jnp.where(lane < 96, pieces[0][:, 8:], pieces[1][:, 8:])
-                stat[xd, at] = jnp.where(lane < 64, low, high)
+                    pieces.append(tops[pl.ds(start, 32, stride=16), :])
+                for spot in range(8):
+                    top = pieces[spot % 2][spot // 2 * 8:spot // 2 * 8 + 8]
+                    tile = top if tile is None else jnp.where(lane >= r * 64 + spot * 8, top, tile)
+            stat[xd, xg] = tile
         at = pl.ds(4 * xg, 4)
         for j in range(1, NX):
             xd = around(x + j, NX)
-            go(sent(stat.at[xd, at], got_stat.at[j - 1, at], hs.at[j - 1, xg], hr.at[j - 1, xg], xpeers[j - 1]))
+            go(sent(stat.at[xd, xg], got_stat.at[j - 1, xg], hs.at[j - 1, xg], hr.at[j - 1, xg], xpeers[j - 1]))
             go(sent(part.at[xd, at], got.at[j - 1, at], gs.at[j - 1, xg], gr.at[j - 1, xg], xpeers[j - 1]))
 
-    def along(slot, value, level):
+    def along(slot):
         peer = {"z": jnp.int32(slot)}
         return [
             sent(send_stat.at[slot], land_stat.at[z], ts.at[slot], tr.at[z], peer),
@@ -261,26 +267,26 @@
         ]
 
     def combine(xg):
-        at = pl.ds(4 * xg, 4)
         for j in range(NX - 1):
-            arrived(got_stat.at[j, at], hr.at[j, xg])
-            arrived(got.at[j, at], gr.at[j, xg])
-        for slot in range(4 * xg, 4 * xg + 4):
-            items = [(part[x, slot].astype(jnp.float32), stat[x, slot])]
-            for j in range(NX - 1):
-                items.append((got[j, slot].astype(jnp.float32), got_stat[j, slot]))
-            value, level = blended(items)
+            arrived(got_stat.at[j, xg], hr.at[j, xg])
+            arrived(got.at[j, pl.ds(4 * xg, 4)], gr.at[j, xg])
+        shares, level = weighed([stat[x, xg]] + [got_stat[j, xg] for j in range(NX - 1)])
+        for i in range(4):
+            slot = 4 * xg + i
+            items = [part[x, slot]] + [got[j, slot] for j in range(NX - 1)]
+            value = mixed_by([item.astype(jnp.float32) for item in items], shares, 32 * i)
+            turned = pltpu.roll(level, 128 - 32 * i, 1) if i else level
 
             @pl.when(z == slot)
-            def _(value=value, level=level):
+            def _(value=value, turned=turned):
                 land[z] = value.astype(jnp.bfloat16)
-                land_stat[z] = level
+                land_stat[z] = turned
 
             @pl.when(z != slot)
-            def _(value=value, level=level, slot=slot):
+            def _(value=value, turned=turned, slot=slot):
                 send[slot] = value.astype(jnp.bfloat16)
-                send_stat[slot] = level
-                for copy in along(slot, value, level):
+                send_stat[slot] = turned
+                for copy in along(slot):
                     copy.start()
 
     group(0)
@@ -295,29 +301,48 @@
         slot = around(z - hop, NZ)
         arrived(land_stat.at[slot], tr.at[slot])
         arrived(land.at[slot], rr.at[slot])
-    items = [(land[slot].astype(jnp.float32), land_stat[slot]) for slot in range(NZ)]
-    merged[z] = blended(items)[0].astype(jnp.bfloat16)
+    shares, _ = weighed([land_stat[slot] for slot in range(NZ)])
+    merged[z] = mixed_by([land[slot].astype(jnp.float32) for slot in range(NZ)], shares, 0).astype(jnp.bfloat16)
     for hop in nearest(True):
         go(sent(merged.at[z], merged.at[z], ms.at[hop], mr.at[hop], {"z": around(z + hop, NZ)}))
-    for number, peer in enumerate(near):
+    for peer in near:
         there = peer["x"] * 2 + peer["c"]
-        for n in range(2):
-            arrived(wz.at[there, pl.ds(64 * n, 64), pl.ds(256 * n, 256)], wr.at[there, n])
-    for hop in nearest():
-        arrived(merged.at[around(z - hop, NZ)], mr.at[hop])
-    rows = merged[...].reshape(NY, 2, 32, 256)
-    rows = jnp.concatenate([rows[:, 0].reshape(128, 256), rows[:, 1].reshape(128, 256)], axis=1)
+        arrived(wz.at[there, pl.ds(0, 64), pl.ds(0, 256)], wr.at[there])
     for spot in range(2 * NX):
-        term = lax.dot_general(rows, wz[spot], (((1,), (1,)), ((), ())), preferred_element_type=jnp.float32)
-        terms[spot] = term.reshape(NY, 32, 128).astype(TERM)
-    number = 0
-    for j in range(NY)[::-1]:
-        for peer in ([] if j == 0 else [{"x": x, "c": c}]) + near:
-            yd = around(y + j, NY)
-            spot = peer["x"] * 2 + peer["c"]
-            mark = y * 8 + here
-            go(sent(terms.at[spot, yd], terms_in.at[mark], fs.at[number], fr.at[mark], {"y": yd, **peer}))
-            number += 1
+        wz[spot, 64:, 256:] = wz[spot, :64, :256]
+
+    def outward(rows_of, number):
+        peer = around_me[number]
+        spot = peer["x"] * 2 + peer["c"]
+        mark = y * 8 + here
+        return sent(
+            terms.at[spot, rows_of], terms_in.at[mark], fs.at[rows_of, number], fr.at[mark], {"y": rows_of, **peer}
+        )
+
+    for turn in (0, 1, 3, 2):
+        rows_of = around(lax.div(z, NX) + turn, NY)
+        for i in range(4):
+            slot = rows_of * 4 + i
+            hop = around(z - slot + NZ, NZ)
+            if turn == 0:
+
+                @pl.when(hop != 0)
+                def _(slot=slot, hop=hop):
+                    arrived(merged.at[slot], mr.at[hop])
+            else:
+                arrived(merged.at[slot], mr.at[hop])
+        rows = merged[pl.ds(rows_of * 4, 4)].reshape(2, 32, 256)
+        rows = jnp.concatenate([rows[0], rows[1]], axis=1)
+        for spot in range(2 * NX):
+            term = lax.dot_general(rows, wz[spot], (((1,), (1,)), ((), ())), preferred_element_type=jnp.float32)
+            terms[spot, rows_of] = term.astype(TERM)
+
+        @pl.when(rows_of != y)
+        def _(rows_of=rows_of):
+            outward(rows_of, 0).start()
+
+        for number in range(1, 8):
+            outward(rows_of, number).start()
     total = terms[here, y].astype(jnp.float32)
     for j in range(NY):
         for peer in ([] if j == 0 else [{"x": x, "c": c}]) + near:
@@ -329,35 +354,46 @@
     result[...] = lines[:, :64].astype(jnp.bfloat16)
     for copy in started:
         copy.wait_send()
+    for rows_of in range(NY):
+
+        @pl.when(rows_of != y)
+        def _(rows_of=rows_of):
+            outward(rows_of, 0).wait_send()
+
+        for number in range(1, 8):
+            outward(rows_of, number).wait_send()
     for slot in range(NZ):
 
         @pl.when(z != slot)
         def _(slot=slot):
-            for copy in along(slot, None, None):
+            for copy in along(slot):
                 copy.wait_send()
 
 
 def step(select, table, block_page, q, k, v, w):
     anywhere = pl.BlockSpec(memory_space=pl.ANY)
     inside = pl.BlockSpec(memory_space=VMEM)
-    scalars = pl.BlockSpec(memory_space=pltpu.MemorySpace.SMEM)
     half = lambda *shape: pltpu.VMEM(shape, jnp.bfloat16)
     full = lambda *shape: pltpu.VMEM(shape, jnp.float32)
     pages = (PAGES_DEV, 2 * PAGE, HEAD)
     return pl.pallas_call(
         step_kernel,
         out_shape=jax.ShapeDtypeStruct((64, 64), jnp.bfloat16),
-        in_specs=[scalars] * 3 + [inside] + [anywhere] * 3,
+        in_specs=[anywhere] * 7,
         out_specs=inside,
         scratch_shapes=[
+            pltpu.SMEM(select.shape, jnp.int32),
+            pltpu.SMEM(table.shape, jnp.int32),
+            pltpu.SMEM(block_page.shape, jnp.int32),
             pltpu.SMEM((BLOCKS * 2 * 8,), jnp.int32),
+            half(2, 16, HEAD),
             half(NX, NZ, 2, 16, HEAD),
             half(*pages), half(*pages), half(*pages), half(*pages),
             full(4, 2 * PAGE, HEAD),
             half(4, KEYS, HEAD), half(4, KEYS, HEAD),
             full(512, HEAD), full(512, HEAD),
-            half(NX, NZ, 16, 256), full(NX, NZ, 8, HEAD),
-            half(NX - 1, NZ, 16, 256), full(NX - 1, NZ, 8, HEAD),
+            half(NX, NZ, 16, 256), full(NX, NX, 8, HEAD),
+            half(NX - 1, NZ, 16, 256), full(NX - 1, NX, 8, HEAD),
             half(NZ, 16, 256), full(NZ, 8, HEAD),
             half(NZ, 16, 256), full(NZ, 8, HEAD),
             half(NZ, 16, 256),
@@ -365,13 +401,13 @@
             pltpu.VMEM((2 * NX, NY, 32, 128), TERM),
             pltpu.VMEM((8 * NY, 32, 128), TERM),
             full(64, 128),
-            DMA((5,)), DMA((2,)), DMA((2,)),
+            DMA((8,)), DMA((2,)), DMA((2,)),
             DMA((NZ, 2)), DMA((NZ, 2)), DMA((NX - 1, NZ)), DMA((NX - 1, NZ)),
-            DMA((7, 2)), DMA((8, 2)),
+            DMA((7,)), DMA((8,)),
             DMA((NX - 1, NX)), DMA((NX - 1, NX)), DMA((NX - 1, NX)), DMA((NX - 1, NX)),
             DMA((NZ,)), DMA((NZ,)), DMA((NZ,)), DMA((NZ,)),
             DMA((NZ,)), DMA((NZ,)),
-            DMA((31,)), DMA((32,)),
+            DMA((NY, 8)), DMA((32,)),
         ],
         compiler_params=pltpu.CompilerParams(collective_id=0, has_side_effects=True),
         name="step",

time: 83.7 us -> 77.1 us (0.921)
  the two profiles are of different devices: /device:TPU:1 before, /device:TPU:17 now
where the time goes in v1:
time: 77.1 us; the launch traced here: 76.8 us
  Pallas kernels  75.5 us (98%)
  local copies, waits for them, and re-layouts  1.32 us (2%)
    pallas_call x1, Pallas kernels, step(): pl.pallas_call(step_kernel, out_shape=jax.ShapeDtypeStruct((64, 64), jnp....  75.5 us

profile of v1, /device:TPU:17, one launch (start us, length us, event | category | flops | bytes accessed | tf_op | source)
XLA Modules:
  0.0 76.8 jit_solution(583800030067822122)
XLA Ops:
  0.0 75.5 %step.1 = bf16[64,64]{1,0:T(8,128)(2,1)} custom-call(s32[2,24]{1,0:T(2,128)} %select_in.1, s32[2048]{0:T(1024)} %table_in.1, s32[2]{0:T(128)} %block_page_in.1, bf16[2,16,128]{2,1,0:T(8,128)(2,1)} %bitcast.11, bf16[16,256,128]{2,1,0:T(8,128)(2,1)} %bitcast.8, bf16[16,256,128]{2,1,0:T(8,128)(2,1)} %bitcast.9, bf16[64,2048]{1,0:T(8,128)(2,1)} %bitcast.10), custom_call_target="tpu_custom_call" | custom-call | tf_op jit(solution)/shard_map/step/pallas_call | solution.py:379
  75.5 1.3 %copy.10 = bf16[64,64]{1,0:T(8,128)(2,1)} copy(bf16[64,64]{1,0:T(8,128)(2,1)} %step.1) | data formatting | bytes 16384

commit v2 on v1

--- a/solution.py
+++ b/solution.py
@@ -9,6 +9,7 @@
 PAGES = ("x", "z", "c")
 MESH = pl.DeviceIdType.MESH
 NX, NZ, NY = 4, 16, 4
+REACH = NZ // 4
 PAGE = 128
 PAGES_DEV = 16
 PICKED = 6
@@ -17,6 +18,7 @@
 HEAD = 128
 KEYS = PICKED * PAGE
 SCALE = HEAD ** -0.5
+SCALE2 = SCALE * 1.4426950408889634
 FLOOR = -1e30
 VMEM = pltpu.MemorySpace.VMEM
 DMA = pltpu.SemaphoreType.DMA
@@ -125,7 +127,8 @@
     xpeers = [{"x": around(x + j, NX)} for j in range(1, NX)]
     around_me = [{"x": around(x + j, NX), "c": lax.rem(c + d, 2)} for j in range(NX) for d in range(2)]
     near = around_me[1:]
-    peers = [{"z": around(z + hop, NZ), "c": core} for hop in nearest(True) for core in range(2)] + near
+    close = nearest()[2 * REACH - 1::-1]
+    peers = [{"z": around(z + hop, NZ), "c": core} for hop in close for core in range(2)] + near
     for j in range(1, NY):
         for peer in around_me:
             peers.append({"y": around(y + j, NY), **peer})
@@ -142,16 +145,10 @@
     ]
     for copy in own:
         copy.start()
-    for copy in own[:4]:
-        copy.wait()
+    own[3].wait()
     copy = pltpu.make_async_copy(q.at[c], qall.at[x, z, c], ls.at[7])
     copy.start()
-    zero = jnp.zeros((2 * NX, 64, 256), jnp.bfloat16)
-    wz[:, :64, 256:] = zero
-    wz[:, 64:, :256] = zero
-    listed(select, table, block_page, lists, x * NZ + z, c)
-    for copy in own[4:] + [copy]:
-        copy.wait()
+    own.append(copy)
     started = []
 
     def go(copy):
@@ -170,31 +167,58 @@
                 for n, (raw, kept) in enumerate(zip(raws, (keys, values))):
                     spot = block * 2 + n
                     flat[spot] = raw[row].astype(jnp.float32)
-                    kept[block * 2 + side, at, :] = flat[spot, pl.ds(c, PAGE, stride=2), :].astype(jnp.bfloat16)
+                    kept[block * 2 + side, at, :HEAD] = flat[spot, pl.ds(c, PAGE, stride=2), :].astype(jnp.bfloat16)
             return 0
 
         lax.fori_loop(0, PICKED, one, 0)
 
-    untangle(0, (knear, vnear))
     wait_for_all()
-    for hop in nearest(True):
+    for hop in close:
         for core in range(2):
             peer = {"z": around(z + hop, NZ), "c": core}
             go(sent(q.at[core], qall.at[x, z, c], zs.at[hop, core], zr.at[hop, c], peer))
     go(sent(q.at[1 - c], qall.at[x, z, c], zs.at[0, 0], zr.at[0, c], other))
+    own[4].wait()
+    own[5].wait()
     go(sent(knear, kfar, ps.at[0], pr.at[0], other))
     go(sent(vnear, vfar, ps.at[1], pr.at[1], other))
     for number, peer in enumerate(near):
         theirs = pl.multiple_of((peer["c"] * NX + peer["x"]) * 256, 256)
         target = wz.at[here, pl.ds(0, 64), pl.ds(0, 256)]
         go(sent(w.at[:, pl.ds(theirs, 256)], target, ws.at[number], wr.at[here], peer))
+    for copy in own[:3] + own[6:]:
+        copy.wait()
+    def came(hop):
+        slot = around(z - hop, NZ)
+        for core in range(2):
+            arrived(qall.at[x, slot, core], zr.at[hop, core])
+        return slot
+
+    for sign in (1, -1):
+        slot = came(REACH if sign == 1 else NZ - REACH)
+        for leg in range(REACH if sign == 1 else REACH - 1, 0, -1):
+            hop = sign * (REACH + leg) % NZ
+            go(sent(
+                qall.at[x, slot], qall.at[x, slot], zs.at[hop, 0], zr.at[hop, 0], {"z": around(z + sign * leg, NZ)}
+            ))
     arrived(qall.at[x, z, 1 - c], zr.at[0, 1 - c])
     across(z, 0)
-    for number, hop in enumerate(nearest()):
+    for number, hop in enumerate(nearest()[:2 * REACH]):
+        if hop in (REACH, NZ - REACH):
+            slot = around(z - hop, NZ)
+        else:
+            slot = came(hop)
+        across(slot, 1 + number)
+    zero = jnp.zeros((2 * NX, 64, 256), jnp.bfloat16)
+    wz[:, :64, 256:] = zero
+    wz[:, 64:, :256] = zero
+    values[:, :, HEAD:] = jnp.ones((4, KEYS, HEAD), jnp.bfloat16)
+    listed(select, table, block_page, lists, x * NZ + z, c)
+    untangle(0, (knear, vnear))
+    for number, hop in enumerate(nearest()[2 * REACH:]):
         slot = around(z - hop, NZ)
-        arrived(qall.at[x, slot, 0], zr.at[hop, 0])
-        arrived(qall.at[x, slot, 1], zr.at[hop, 1])
-        across(slot, 1 + number)
+        arrived(qall.at[x, slot], zr.at[hop, 0])
+        across(slot, 1 + 2 * REACH + number)
     arrived(kfar, pr.at[0])
     arrived(vfar, pr.at[1])
     untangle(1, (kfar, vfar))
@@ -226,9 +250,9 @@
                 first = jnp.where(key <= row + slack, scores[:, :PAGE], FLOOR)
                 scores = jnp.concatenate([first, scores[:, PAGE:]], axis=1)
                 peak = jnp.max(scores, axis=1, keepdims=True)
-                weights = jnp.exp((scores - peak) * SCALE)
-                total = jnp.sum(weights, axis=1, keepdims=True)
-                out = jnp.dot(weights.astype(jnp.bfloat16), values[combo], preferred_element_type=jnp.float32)
+                weights = jnp.exp2((scores - peak) * SCALE2)
+                both = jnp.dot(weights.astype(jnp.bfloat16), values[combo], preferred_element_type=jnp.float32)
+                out, total = both[:, :HEAD], both[:, HEAD:HEAD + 1]
                 level = peak * SCALE + jnp.log(total)
                 level = jnp.where(lists[combo * 8 + PICKED] == PICKED, level, FLOOR)
                 sides.append((out, total, level))
@@ -390,7 +414,7 @@
             half(NX, NZ, 2, 16, HEAD),
             half(*pages), half(*pages), half(*pages), half(*pages),
             full(4, 2 * PAGE, HEAD),
-            half(4, KEYS, HEAD), half(4, KEYS, HEAD),
+            half(4, KEYS, HEAD), half(4, KEYS, 2 * HEAD),
             full(512, HEAD), full(512, HEAD),
             half(NX, NZ, 16, 256), full(NX, NX, 8, HEAD),
             half(NX - 1, NZ, 16, 256), full(NX - 1, NX, 8, HEAD),

time: 77.1 us -> 73.9 us (0.958)
  Pallas kernels: 75.5 us -> 72.4 us
    pallas_call x1, Pallas kernels: 75.5 us -> 72.4 us  [step(): pl.pallas_call(step_kernel, out_shape=jax.ShapeDtypeStruct((64, 64), jnp....]
where the time goes in v2:
time: 73.9 us; the launch traced here: 73.7 us
  Pallas kernels  72.4 us (98%)
  local copies, waits for them, and re-layouts  1.32 us (2%)
    pallas_call x1, Pallas kernels, step(): pl.pallas_call(step_kernel, out_shape=jax.ShapeDtypeStruct((64, 64), jnp....  72.4 us

profile of v2, /device:TPU:17, one launch (start us, length us, event | category | flops | bytes accessed | tf_op | source)
XLA Modules:
  0.0 73.7 jit_solution(10658972629556563961)
XLA Ops:
  0.0 72.4 %step.1 = bf16[64,64]{1,0:T(8,128)(2,1)} custom-call(s32[2,24]{1,0:T(2,128)} %select_in.1, s32[2048]{0:T(1024)} %table_in.1, s32[2]{0:T(128)} %block_page_in.1, bf16[2,16,128]{2,1,0:T(8,128)(2,1)} %bitcast.11, bf16[16,256,128]{2,1,0:T(8,128)(2,1)} %bitcast.8, bf16[16,256,128]{2,1,0:T(8,128)(2,1)} %bitcast.9, bf16[64,2048]{1,0:T(8,128)(2,1)} %bitcast.10), custom_call_target="tpu_custom_call" | custom-call | tf_op jit(solution)/shard_map/step/pallas_call | solution.py:403
  72.4 1.3 %copy.10 = bf16[64,64]{1,0:T(8,128)(2,1)} copy(bf16[64,64]{1,0:T(8,128)(2,1)} %step.1) | data formatting | bytes 16384

commit v3 on v2

--- a/solution.py
+++ b/solution.py
@@ -188,6 +188,11 @@
         go(sent(w.at[:, pl.ds(theirs, 256)], target, ws.at[number], wr.at[here], peer))
     for copy in own[:3] + own[6:]:
         copy.wait()
+    zero = jnp.zeros((2 * NX, 64, 256), jnp.bfloat16)
+    wz[:, :64, 256:] = zero
+    wz[:, 64:, :256] = zero
+    values[:, :, HEAD:] = jnp.ones((4, KEYS, HEAD), jnp.bfloat16)
+    listed(select, table, block_page, lists, x * NZ + z, c)
     def came(hop):
         slot = around(z - hop, NZ)
         for core in range(2):
@@ -209,11 +214,6 @@
         else:
             slot = came(hop)
         across(slot, 1 + number)
-    zero = jnp.zeros((2 * NX, 64, 256), jnp.bfloat16)
-    wz[:, :64, 256:] = zero
-    wz[:, 64:, :256] = zero
-    values[:, :, HEAD:] = jnp.ones((4, KEYS, HEAD), jnp.bfloat16)
-    listed(select, table, block_page, lists, x * NZ + z, c)
     untangle(0, (knear, vnear))
     for number, hop in enumerate(nearest()[2 * REACH:]):
         slot = around(z - hop, NZ)

time: 73.9 us -> 73.9 us (level)
  no operation moved by 1% of the time
where the time goes in v3:
time: 73.9 us; the launch traced here: 73.7 us
  Pallas kernels  72.4 us (98%)
  local copies, waits for them, and re-layouts  1.32 us (2%)
    pallas_call x1, Pallas kernels, step(): pl.pallas_call(step_kernel, out_shape=jax.ShapeDtypeStruct((64, 64), jnp....  72.4 us

profile of v3, /device:TPU:17, one launch (start us, length us, event | category | flops | bytes accessed | tf_op | source)
XLA Modules:
  0.0 73.7 jit_solution(14656760714883168717)
XLA Ops:
  0.0 72.4 %step.1 = bf16[64,64]{1,0:T(8,128)(2,1)} custom-call(s32[2,24]{1,0:T(2,128)} %select_in.1, s32[2048]{0:T(1024)} %table_in.1, s32[2]{0:T(128)} %block_page_in.1, bf16[2,16,128]{2,1,0:T(8,128)(2,1)} %bitcast.11, bf16[16,256,128]{2,1,0:T(8,128)(2,1)} %bitcast.8, bf16[16,256,128]{2,1,0:T(8,128)(2,1)} %bitcast.9, bf16[64,2048]{1,0:T(8,128)(2,1)} %bitcast.10), custom_call_target="tpu_custom_call" | custom-call | tf_op jit(solution)/shard_map/step/pallas_call | solution.py:403
  72.4 1.3 %copy.10 = bf16[64,64]{1,0:T(8,128)(2,1)} copy(bf16[64,64]{1,0:T(8,128)(2,1)} %step.1) | data formatting | bytes 16384
